TPU v7x, 256 devices: a whole 4x4x8 slice. The times are simulated.
256 devices in a mesh: src: 32 (over y, z), tm: 8 (over x, core).
Axes of the slice: x: 4, y: 4, z: 8, core: 2. Of those that a mesh axis runs over, the one named last changes fastest.
Arguments:
- green: bfloat16 [8, 4096, 128, 128], P('tm', 'src'), may hold values from -0.046875 to 0.046875
- block_rows: int32 [8, 4096], P('tm', 'src'), may hold values from 0 to 31
- block_cols: int32 [8, 4096], P('tm', 'src'), may hold values from 0 to 31
- block_live: int32 [8, 4096], P('tm', 'src'), may hold values from 0 to 1, as said below
- data: float32 [8, 4096, 128], P('tm', 'src'), may hold values from -6 to 6
- row_weight: float32 [8, 4096], P('tm', 'src'), may hold values from 0.3 to 9
- source_gain: float32 [131072], P('src'), may hold values from 0.2 to 3
Outputs:
- solution: float32 [131072, 128], P(('src', 'tm'))
- residual: float32 [8, 4096, 128], P('tm', 'src')
- misfit: float32 [2, 128], replicated
Inputs may be any that keep to these rules, and one draw needn't show every extreme that they name: `block_live`: within one device's 128 slots every slot is live with the same chance, a chance that differs from device to device; in some device all 128 slots are live.
All inputs are finite; a program needn't handle non-finite values.
Results may differ from a plain program's by a relative error of at most 0.0038.
Values may be sent and summed in bfloat16 or wider, within the bound.
A program may use at most 128 MiB of HBM per device.

v0:
```python
import jax
import jax.numpy as jnp
from jax import lax
from jax.sharding import PartitionSpec as P

ITERS = 2
HIGH = lax.Precision.HIGHEST
EPSILON = 1e-06


def shards(green, block_rows, block_cols, block_live, data, row_weight, source_gain):
    blocks = green[0]
    slot_count = blocks.shape[0]
    block_size = blocks.shape[1]
    datasets = data.shape[2]
    own_rows = data.shape[1]
    own_blocks = own_rows // block_size
    groups = lax.axis_size("src")
    windows = lax.axis_size("tm")
    window_blocks = own_blocks * groups
    sources = source_gain.shape[0]
    col_blocks = sources // block_size
    share_rows = sources // windows
    total_rows = own_rows * groups * windows
    live_slots = block_live[0].astype(jnp.float32)[:, None]
    row_hit = block_rows[0][:, None] == jnp.arange(window_blocks, dtype=jnp.int32)[None, :]
    col_hit = block_cols[0][:, None] == jnp.arange(col_blocks, dtype=jnp.int32)[None, :]
    gather_rows = row_hit.astype(jnp.bfloat16)
    gather_cols = col_hit.astype(jnp.bfloat16)
    spread_rows = jnp.transpose(row_hit.astype(jnp.float32) * live_slots)
    spread_cols = jnp.transpose(col_hit.astype(jnp.float32) * live_slots)
    weight = row_weight[0][:, None]
    tm_index = lax.axis_index("tm")
    gain_group = source_gain[:, None]

    def adjoint(residual):
        sent = (weight * residual).astype(jnp.bfloat16).reshape(own_blocks, block_size * datasets)
        gathered = lax.all_gather(sent, "src", axis=0, tiled=True)
        picked = jnp.dot(gather_rows, gathered, preferred_element_type=jnp.bfloat16)
        products = jnp.einsum(
            "kac,kar->kcr",
            blocks,
            picked.reshape(slot_count, block_size, datasets),
            preferred_element_type=jnp.float32,
        )
        products = products.reshape(slot_count, block_size * datasets)
        return jnp.dot(spread_cols, products, precision=HIGH).reshape(sources, datasets)

    def steepest_of(residual):
        summed = lax.psum(adjoint(residual), "tm")
        steepest = gain_group * summed
        gamma_now = lax.psum(jnp.sum(steepest * steepest, axis=0), "src")
        return (steepest, gamma_now)

    residual = weight * data[0]
    steepest, gamma_now = steepest_of(residual)
    direction = steepest
    solution = jnp.zeros((share_rows, datasets), jnp.float32)
    misfits = []
    for iteration in range(ITERS):
        forward_picked = jnp.dot(
            gather_cols,
            (gain_group * direction)
            .astype(jnp.bfloat16)
            .reshape(col_blocks, block_size * datasets),
            preferred_element_type=jnp.bfloat16,
        )
        forward_products = jnp.einsum(
            "kac,kcr->kar",
            blocks,
            forward_picked.reshape(slot_count, block_size, datasets),
            preferred_element_type=jnp.float32,
        )
        forward_products = forward_products.reshape(slot_count, block_size * datasets)
        forward_summed = lax.psum_scatter(
            jnp.dot(spread_rows, forward_products, precision=HIGH),
            "src",
            scatter_dimension=0,
            tiled=True,
        )
        image = weight * forward_summed.reshape(own_rows, datasets)
        image_norm = lax.psum(jnp.sum(image * image, axis=0), ("src", "tm"))
        step_size = gamma_now / (image_norm + EPSILON)
        solution = solution + step_size * lax.dynamic_slice_in_dim(
            direction, tm_index * share_rows, share_rows, 0
        )
        residual = residual - step_size * image
        misfits.append(lax.psum(jnp.sum(residual * residual, axis=0), ("src", "tm")) / total_rows)
        if iteration + 1 < ITERS:
            steepest, gamma_next = steepest_of(residual)
            direction = steepest + gamma_next / (gamma_now + EPSILON) * direction
            gamma_now = gamma_next
    return (solution, residual[None], jnp.stack(misfits))


def solution(mesh):
    placed = (
        P("tm", "src", None, None),
        P("tm", "src"),
        P("tm", "src"),
        P("tm", "src"),
        P("tm", "src", None),
        P("tm", "src"),
        P("src"),
    )
    return jax.shard_map(
        shards,
        mesh=mesh,
        in_specs=placed,
        out_specs=(P(("src", "tm"), None), P("tm", "src", None), P()),
        check_vma=False,
    )
```

profile of v0, /device:TPU:1, one launch (start us, length us, event | category | flops | bytes accessed | tf_op | source)
XLA Modules:
  0.0 1052.1 jit_solution(14238654614562010378)
XLA Ops:
  10.2 78.8 %all-gather.5.cloned.1.call-done = bf16[32,1,16384]{2,1,0:T(2,128)(2,1)} async-done(((bf16[1,1,16384]{2,1,0:T(2,128)(2,1)}), bf16[32,1,16384]{2,1,0:T(2,128)(2,1)}) %all-gather.5.cloned.1.call-update) | async-done | bytes 1048592 | tf_op jit(solution)/shard_map/all_gather | solution.py:38
  89.1 3.2 convolution_bitcast_fusion.1
  94.5 4.8 fusion.10
  99.2 9.3 copy.27
  108.6 10.7 %fusion.43 = f32[32,16384]{1,0:T(8,128)S(1)} fusion(f32[128,16384]{0,1:T(8,128)} %bitcast.97, f32[128]{0:T(128)S(1)} %convert_bitcast_fusion.2, s32[128]{0:T(128)S(1)} %bitcast.117), kind=kOutput, calls=%fused_computation.48 | convolution fusion | flops 805314560 | bytes 10486784 | tf_op jit(solution)/shard_map/dot_general | solution.py:47
  121.3 69.5 %all-reduce.8.cloned.1.call-done = f32[4096,128]{1,0:T(8,128)} async-done(((f32[4096,128]{1,0:T(8,128)}), f32[4096,128]{1,0:T(8,128)}) %all-reduce.8.cloned.1.call-update) | async-done | bytes 2097168 | tf_op jit(solution)/shard_map/psum | solution.py:50
  190.9 1.9 multiply_convert_fusion.1
  194.1 2.7 fusion.29
  196.8 7.3 fusion.13
  204.1 9.4 copy.30
  213.4 11.7 %fusion.39 = f32[32,16384]{1,0:T(8,128)} fusion(f32[128,16384]{0,1:T(8,128)} %bitcast.98, s32[128]{0:T(128)S(1)} %bitcast.122, f32[128]{0:T(128)S(1)} %convert_bitcast_fusion.2), kind=kOutput, calls=%fused_computation.44 | convolution fusion | flops 805314560 | bytes 10486784 | tf_op jit(solution)/shard_map/dot_general | solution.py:76
  226.4 61.0 %psum.57 = f32[128]{0:T(128)S(1)} all-reduce(f32[128]{0:T(128)S(1)} %multiply_reduce_fusion.1), channel_id=1, replica_groups=mesh['src'=32,'tm'=8] {'src'}, use_global_device_ids=true, to_apply=%region_2.0 | all-reduce | flops 128 | bytes 1024 | tf_op jit(solution)/shard_map/psum | solution.py:52
  287.4 89.4 %all-reduce.12.cloned.1.call-done = f32[32,16384]{1,0:T(8,128)} async-done(((f32[32,16384]{1,0:T(8,128)}), f32[32,16384]{1,0:T(8,128)}) %all-reduce.12.cloned.1.call-update) | async-done | bytes 2097168
  376.8 1.7 constant_dynamic-slice_fusion.1
  378.6 78.4 %psum.58 = f32[128]{0:T(128)S(1)} all-reduce(f32[128]{0:T(128)S(1)} %multiply_reduce_fusion.5), channel_id=1, replica_groups=mesh['src'=32,'tm'=8] {'src','tm'}, use_global_device_ids=true, to_apply=%region_5.0 | all-reduce | flops 128 | bytes 1024 | tf_op jit(solution)/shard_map/psum | solution.py:82
  457.0 2.4 convert_bitcast_fusion
  459.7 69.4 %all-gather.7.cloned.1.call-done = bf16[32,1,16384]{2,1,0:T(2,128)(2,1)} async-done(((bf16[1,1,16384]{2,1,0:T(2,128)(2,1)}), bf16[32,1,16384]{2,1,0:T(2,128)(2,1)}) %all-gather.7.cloned.1.call-update) | async-done | bytes 1048592 | tf_op jit(solution)/shard_map/all_gather | solution.py:38
  529.1 3.2 convolution_bitcast_fusion
  534.5 4.7 fusion.18
  539.2 9.4 copy.32
  548.6 11.7 %fusion.41 = f32[32,16384]{1,0:T(8,128)} fusion(f32[128,16384]{0,1:T(8,128)} %bitcast.99, f32[128]{0:T(128)S(1)} %convert_bitcast_fusion.2, s32[128]{0:T(128)S(1)} %bitcast.119), kind=kOutput, calls=%fused_computation.46 | convolution fusion | flops 805314560 | bytes 10486784 | tf_op jit(solution)/shard_map/dot_general | solution.py:47
  560.3 2.7 reshape.254
  563.0 70.0 %all-reduce.10.cloned.1.call-done = f32[4096,128]{1,0:T(8,128)} async-done(((f32[4096,128]{1,0:T(8,128)}), f32[4096,128]{1,0:T(8,128)}) %all-reduce.10.cloned.1.call-update) | async-done | bytes 2097168 | tf_op jit(solution)/shard_map/psum | solution.py:50
  633.1 1.9 multiply_reduce_fusion
  635.0 61.2 %psum.60 = f32[128]{0:T(128)S(1)} all-reduce(f32[128]{0:T(128)S(1)} %multiply_reduce_fusion), channel_id=1, replica_groups=mesh['src'=32,'tm'=8] {'src'}, use_global_device_ids=true, to_apply=%region_8.0 | all-reduce | flops 128 | bytes 1024 | tf_op jit(solution)/shard_map/psum | solution.py:52
  696.2 3.3 multiply_convert_fusion
  703.2 7.3 fusion.21
  710.4 9.4 copy.35
  719.8 11.7 %fusion.37 = f32[32,16384]{1,0:T(8,128)} fusion(f32[128,16384]{0,1:T(8,128)} %bitcast.96, s32[128]{0:T(128)S(1)} %bitcast.124, f32[128]{0:T(128)S(1)} %convert_bitcast_fusion.2), kind=kOutput, calls=%fused_computation.42 | convolution fusion | flops 805314560 | bytes 10486784 | tf_op jit(solution)/shard_map/dot_general | solution.py:76
  731.6 157.0 %all-reduce.14.cloned.1.call-done = f32[32,16384]{1,0:T(8,128)} async-done(((f32[32,16384]{1,0:T(8,128)}), f32[32,16384]{1,0:T(8,128)}) %all-reduce.14.cloned.1.call-update) | async-done | bytes 2097168
  890.4 78.4 %psum.61 = f32[128]{0:T(128)S(1)} all-reduce(f32[128]{0:T(128)S(1)} %multiply_reduce_fusion.4), channel_id=1, replica_groups=mesh['src'=32,'tm'=8] {'src','tm'}, use_global_device_ids=true, to_apply=%region_11.0 | all-reduce | flops 128 | bytes 1024 | tf_op jit(solution)/shard_map/psum | solution.py:82
  968.9 73.1 %all-reduce.2 = (f32[128]{0:T(128)S(1)}, f32[128]{0:T(128)S(1)}) all-reduce(f32[128]{0:T(128)S(1)} %get-tuple-element.4, f32[128]{0:T(128)S(1)} %get-tuple-element.3), channel_id=1, replica_groups=mesh['src'=32,'tm'=8] {'src','tm'}, use_global_device_ids=true, to_apply=%region_15.0 | all-reduce | flops 256 | bytes 2048 | tf_op jit(solution)/shard_map/psum | solution.py:88
  (55 shorter events, 21.0 us)
Async XLA Ops:
  7.2 81.9 %all-gather.5.cloned.1.call-start = ((), (), s32[]{:S(2)}) async-start(), calls=%async_computation.2 | async-start | bytes 2162688 | tf_op jit(solution)/shard_map/all_gather | solution.py:38
  9.5 181.3 %all-reduce.8.cloned.1.call-start = ((), (), s32[]{:S(2)}) async-start(), calls=%async_computation | async-start | bytes 4194304 | tf_op jit(solution)/shard_map/psum | solution.py:50
  92.3 2.2 copy-start
  99.2 9.3 copy-start.7
  119.3 71.6 %copy-start.5 = (f32[4096]{0:T(1024)S(1)}, f32[4096]{0:T(1024)}, u32[]{:S(2)}) copy-start(f32[4096]{0:T(1024)} %param.13) | copy-start | bytes 49156
  120.8 256.0 %all-reduce.12.cloned.1.call-start = ((), (), s32[]{:S(2)}) async-start(), calls=%async_computation.4 | async-start | bytes 4194304
  194.1 2.7 copy-start.1
  204.1 9.4 copy-start.8
  213.4 11.8 %copy-start.9 = (u32[256]{0:T(256)S(1)}, u32[256]{0:T(256)}, u32[]{:S(2)}) copy-start(u32[256]{0:T(256)} %constant.28) | copy-start | bytes 3076
  225.1 153.4 %copy-start.6 = (f32[1,128]{1,0:T(1,128)S(1)}, f32[1,128]{1,0:T(1,128)}, u32[]{:S(2)}) copy-start(f32[1,128]{1,0:T(1,128)} %param.12) | copy-start | bytes 1540
  225.2 303.9 %all-gather.7.cloned.1.call-start = ((), (), s32[]{:S(2)}) async-start(), calls=%async_computation.3 | async-start | bytes 2162688 | tf_op jit(solution)/shard_map/all_gather | solution.py:38
  459.5 173.6 %all-reduce.10.cloned.1.call-start = ((), (), s32[]{:S(2)}) async-start(), calls=%async_computation.1 | async-start | bytes 4194304 | tf_op jit(solution)/shard_map/psum | solution.py:50
  532.3 2.2 copy-start.2
  563.0 325.6 %all-reduce.14.cloned.1.call-start = ((), (), s32[]{:S(2)}) async-start(), calls=%async_computation.5 | async-start | bytes 4194304
  701.0 2.2 copy-start.3
  719.8 249.0 %copy-start.4 = (f32[1,128,128]{2,1,0:T(8,128)S(1)}, f32[1,128,128]{2,1,0:T(8,128)}, u32[]{:S(2)}) copy-start(f32[1,128,128]{2,1,0:T(8,128)} %param.11) | copy-start | bytes 196612
Sparse Core Ops, SparseCore 0:
  11.2 77.8 all-gather.4
  120.9 69.8 all-reduce.7
  225.3 151.4 all-reduce.11
  459.6 69.4 all-gather.6
  563.1 69.8 all-reduce.9
  731.7 156.8 all-reduce.13
where the time goes:
time: 1060 us; the launch traced here: 1050 us
  waiting for transfers between devices  534 us (50%)
  blocking collectives  352 us (33%)
  matrix products  80.3 us (8%)
  local copies, waits for them, and re-layouts  54.4 us (5%)
  other arithmetic  15.6 us (1%)
  between operations  14.5 us (1%)
    unnamed x8, waiting for transfers between devices  247 us
    psum x2, blocking collectives, shards(): image_norm = lax.psum(jnp.sum(image * image, axis=0), ('src', 'tm'))  157 us
    all_gather x2, waiting for transfers between devices, adjoint(): gathered = lax.all_gather(sent, 'src', axis=0, tiled=True)  148 us
    psum x2, waiting for transfers between devices, steepest_of(): summed = lax.psum(adjoint(residual), 'tm')  140 us
    psum x2, blocking collectives, steepest_of(): gamma_now = lax.psum(jnp.sum(steepest * steepest, axis=0), 'src')  122 us
    psum x1, blocking collectives, shards(): lax.psum(jnp.sum(residual * residual, axis=0), ('src', 'tm')) / total_rows  73.1 us
    dot_general x2, matrix products, shards(): jnp.dot(spread_rows, forward_products, precision=HIGH)  23.4 us
    dot_general x2, matrix products, adjoint(): jnp.dot(spread_cols, products, precision=HIGH).reshape(sources, datasets)  22.4 us
  transfers between devices with their start and end apart: 6, of which 6 were waited for; matrix products, arithmetic and copies ran while one was open for 0% of the time, Pallas kernels for 0%

commit v1 on v0

--- a/solution.py
+++ b/solution.py
@@ -85,7 +85,10 @@
             direction, tm_index * share_rows, share_rows, 0
         )
         residual = residual - step_size * image
-        misfits.append(lax.psum(jnp.sum(residual * residual, axis=0), ("src", "tm")) / total_rows)
+        misfits.append(
+            jnp.sum(lax.all_gather(jnp.sum(residual * residual, axis=0), ("src", "tm")), 0)
+            / total_rows
+        )
         if iteration + 1 < ITERS:
             steepest, gamma_next = steepest_of(residual)
             direction = steepest + gamma_next / (gamma_now + EPSILON) * direction

time: 1060 us -> 1090 us (1.028)
  blocking collectives: 352 us -> 385 us
    all_gather x0 -> x2, blocking collectives: none -> 106 us  [shards(): lax.all_gather(jnp.sum(residual * residual, axis=0), ('src', 'tm'))]
    psum x1 -> x0, blocking collectives: 73.1 us -> none  [shards(): lax.psum(jnp.sum(residual * residual, axis=0), ('src', 'tm')) / total_rows]
where the time goes in v1:
time: 1090 us
  waiting for transfers between devices  534 us (49%)
  blocking collectives  385 us (35%)
  matrix products  80.3 us (7%)
  local copies, waits for them, and re-layouts  54.4 us (5%)
  other arithmetic  16.2 us (1%)
  between operations  14.5 us (1%)
    unnamed x8, waiting for transfers between devices  247 us
    psum x2, blocking collectives, shards(): image_norm = lax.psum(jnp.sum(image * image, axis=0), ('src', 'tm'))  157 us
    all_gather x2, waiting for transfers between devices, adjoint(): gathered = lax.all_gather(sent, 'src', axis=0, tiled=True)  148 us
    psum x2, waiting for transfers between devices, steepest_of(): summed = lax.psum(adjoint(residual), 'tm')  140 us
    psum x2, blocking collectives, steepest_of(): gamma_now = lax.psum(jnp.sum(steepest * steepest, axis=0), 'src')  122 us
    all_gather x2, blocking collectives, shards(): lax.all_gather(jnp.sum(residual * residual, axis=0), ('src', 'tm'))  106 us
    dot_general x2, matrix products, shards(): jnp.dot(spread_rows, forward_products, precision=HIGH)  23.4 us
    dot_general x2, matrix products, adjoint(): jnp.dot(spread_cols, products, precision=HIGH).reshape(sources, datasets)  22.4 us
  transfers between devices with their start and end apart: 6, of which 6 were waited for; matrix products, arithmetic and copies ran while one was open for 0% of the time, Pallas kernels for 0%

profile of v1, /device:TPU:1, one launch (start us, length us, event | category | flops | bytes accessed | tf_op | source)
XLA Modules:
  0.0 1086.1 jit_solution(1725961482852934098)
XLA Ops:
  10.2 78.8 %all-gather.9.cloned.1.call-done = bf16[32,1,16384]{2,1,0:T(2,128)(2,1)} async-done(((bf16[1,1,16384]{2,1,0:T(2,128)(2,1)}), bf16[32,1,16384]{2,1,0:T(2,128)(2,1)}) %all-gather.9.cloned.1.call-update) | async-done | bytes 1048592 | tf_op jit(solution)/shard_map/all_gather | solution.py:38
  89.1 3.2 convolution_bitcast_fusion.1
  94.5 4.8 fusion.10
  99.2 9.3 copy.27
  108.6 10.7 fusion.43
  121.3 69.5 %all-reduce.7.cloned.1.call-done = f32[4096,128]{1,0:T(8,128)} async-done(((f32[4096,128]{1,0:T(8,128)}), f32[4096,128]{1,0:T(8,128)}) %all-reduce.7.cloned.1.call-update) | async-done | bytes 2097168 | tf_op jit(solution)/shard_map/psum | solution.py:50
  190.9 1.9 multiply_convert_fusion.1
  194.1 2.7 fusion.29
  196.8 7.3 fusion.13
  204.1 9.4 copy.30
  213.4 11.7 %fusion.39 = f32[32,16384]{1,0:T(8,128)} fusion(f32[128,16384]{0,1:T(8,128)} %bitcast.100, s32[128]{0:T(128)S(1)} %bitcast.124, f32[128]{0:T(128)S(1)} %convert_bitcast_fusion.2), kind=kOutput, calls=%fused_computation.44 | convolution fusion | flops 805314560 | bytes 10486784 | tf_op jit(solution)/shard_map/dot_general | solution.py:76
  226.4 61.0 %psum.43 = f32[128]{0:T(128)S(1)} all-reduce(f32[128]{0:T(128)S(1)} %multiply_reduce_fusion.1), channel_id=1, replica_groups=mesh['src'=32,'tm'=8] {'src'}, use_global_device_ids=true, to_apply=%region_2.0 | all-reduce | flops 128 | bytes 1024 | tf_op jit(solution)/shard_map/psum | solution.py:52
  287.4 89.4 %all-reduce.11.cloned.1.call-done = f32[32,16384]{1,0:T(8,128)} async-done(((f32[32,16384]{1,0:T(8,128)}), f32[32,16384]{1,0:T(8,128)}) %all-reduce.11.cloned.1.call-update) | async-done | bytes 2097168
  378.6 78.4 %psum.44 = f32[128]{0:T(128)S(1)} all-reduce(f32[128]{0:T(128)S(1)} %multiply_reduce_fusion.5), channel_id=1, replica_groups=mesh['src'=32,'tm'=8] {'src','tm'}, use_global_device_ids=true, to_apply=%region_5.0 | all-reduce | flops 128 | bytes 1024 | tf_op jit(solution)/shard_map/psum | solution.py:82
  457.0 2.4 convert_bitcast_fusion
  459.7 69.4 %all-gather.11.cloned.1.call-done = bf16[32,1,16384]{2,1,0:T(2,128)(2,1)} async-done(((bf16[1,1,16384]{2,1,0:T(2,128)(2,1)}), bf16[32,1,16384]{2,1,0:T(2,128)(2,1)}) %all-gather.11.cloned.1.call-update) | async-done | bytes 1048592 | tf_op jit(solution)/shard_map/all_gather | solution.py:38
  529.1 3.2 convolution_bitcast_fusion
  534.5 4.7 fusion.18
  539.2 9.4 copy.32
  548.6 11.7 %fusion.41 = f32[32,16384]{1,0:T(8,128)} fusion(f32[128,16384]{0,1:T(8,128)} %bitcast.101, f32[128]{0:T(128)S(1)} %convert_bitcast_fusion.2, s32[128]{0:T(128)S(1)} %bitcast.121), kind=kOutput, calls=%fused_computation.46 | convolution fusion | flops 805314560 | bytes 10486784 | tf_op jit(solution)/shard_map/dot_general | solution.py:47
  560.3 2.7 reshape.272
  563.0 70.1 %all-reduce.9.cloned.1.call-done = f32[4096,128]{1,0:T(8,128)} async-done(((f32[4096,128]{1,0:T(8,128)}), f32[4096,128]{1,0:T(8,128)}) %all-reduce.9.cloned.1.call-update) | async-done | bytes 2097168 | tf_op jit(solution)/shard_map/psum | solution.py:50
  633.1 1.9 multiply_reduce_fusion
  635.1 61.2 %psum.46 = f32[128]{0:T(128)S(1)} all-reduce(f32[128]{0:T(128)S(1)} %multiply_reduce_fusion), channel_id=1, replica_groups=mesh['src'=32,'tm'=8] {'src'}, use_global_device_ids=true, to_apply=%region_8.0 | all-reduce | flops 128 | bytes 1024 | tf_op jit(solution)/shard_map/psum | solution.py:52
  696.3 3.3 multiply_convert_fusion
  703.2 7.3 fusion.21
  710.5 9.4 copy.35
  719.9 11.7 %fusion.37 = f32[32,16384]{1,0:T(8,128)} fusion(f32[128,16384]{0,1:T(8,128)} %bitcast.98, s32[128]{0:T(128)S(1)} %bitcast.126, f32[128]{0:T(128)S(1)} %convert_bitcast_fusion.2), kind=kOutput, calls=%fused_computation.42 | convolution fusion | flops 805314560 | bytes 10486784 | tf_op jit(solution)/shard_map/dot_general | solution.py:76
  731.6 157.0 %all-reduce.13.cloned.1.call-done = f32[32,16384]{1,0:T(8,128)} async-done(((f32[32,16384]{1,0:T(8,128)}), f32[32,16384]{1,0:T(8,128)}) %all-reduce.13.cloned.1.call-update) | async-done | bytes 2097168
  890.5 78.4 %psum.47 = f32[128]{0:T(128)S(1)} all-reduce(f32[128]{0:T(128)S(1)} %multiply_reduce_fusion.4), channel_id=1, replica_groups=mesh['src'=32,'tm'=8] {'src','tm'}, use_global_device_ids=true, to_apply=%region_11.0 | all-reduce | flops 128 | bytes 1024 | tf_op jit(solution)/shard_map/psum | solution.py:82
  969.0 53.3 %all-gather.5 = f32[256,1,128]{2,1,0:T(1,128)S(1)} all-gather(f32[1,1,128]{2,1,0:T(1,128)S(1)} %bitcast.128), channel_id=3, replica_groups=mesh['src'=32,'tm'=8] {'src','tm'}, dimensions={0}, use_global_device_ids=true | all-gather | bytes 131584 | tf_op jit(solution)/shard_map/all_gather | solution.py:89
  1022.6 53.2 %all-gather.4 = f32[256,1,128]{2,1,0:T(1,128)S(1)} all-gather(f32[1,1,128]{2,1,0:T(1,128)S(1)} %bitcast.127), channel_id=2, replica_groups=mesh['src'=32,'tm'=8] {'src','tm'}, dimensions={0}, use_global_device_ids=true | all-gather | bytes 131584 | tf_op jit(solution)/shard_map/all_gather | solution.py:89
  (59 shorter events, 23.3 us)
Async XLA Ops:
  7.2 81.9 %all-gather.9.cloned.1.call-start = ((), (), s32[]{:S(2)}) async-start(), calls=%async_computation.2 | async-start | bytes 2162688 | tf_op jit(solution)/shard_map/all_gather | solution.py:38
  9.5 181.3 %all-reduce.7.cloned.1.call-start = ((), (), s32[]{:S(2)}) async-start(), calls=%async_computation | async-start | bytes 4194304 | tf_op jit(solution)/shard_map/psum | solution.py:50
  92.3 2.2 copy-start
  99.2 9.3 copy-start.7
  119.3 71.6 %copy-start.5 = (f32[4096]{0:T(1024)S(1)}, f32[4096]{0:T(1024)}, u32[]{:S(2)}) copy-start(f32[4096]{0:T(1024)} %param.13) | copy-start | bytes 49156
  120.8 256.0 %all-reduce.11.cloned.1.call-start = ((), (), s32[]{:S(2)}) async-start(), calls=%async_computation.4 | async-start | bytes 4194304
  194.1 2.7 copy-start.1
  204.1 9.4 copy-start.8
  213.4 11.8 %copy-start.9 = (u32[256]{0:T(256)S(1)}, u32[256]{0:T(256)}, u32[]{:S(2)}) copy-start(u32[256]{0:T(256)} %constant.28) | copy-start | bytes 3076
  225.1 153.4 %copy-start.6 = (f32[1,128]{1,0:T(1,128)S(1)}, f32[1,128]{1,0:T(1,128)}, u32[]{:S(2)}) copy-start(f32[1,128]{1,0:T(1,128)} %param.12) | copy-start | bytes 1540
  225.2 303.9 %all-gather.11.cloned.1.call-start = ((), (), s32[]{:S(2)}) async-start(), calls=%async_computation.3 | async-start | bytes 2162688 | tf_op jit(solution)/shard_map/all_gather | solution.py:38
  459.5 173.7 %all-reduce.9.cloned.1.call-start = ((), (), s32[]{:S(2)}) async-start(), calls=%async_computation.1 | async-start | bytes 4194304 | tf_op jit(solution)/shard_map/psum | solution.py:50
  532.3 2.2 copy-start.2
  563.0 325.7 %all-reduce.13.cloned.1.call-start = ((), (), s32[]{:S(2)}) async-start(), calls=%async_computation.5 | async-start | bytes 4194304
  701.1 2.2 copy-start.3
  719.9 249.0 %copy-start.4 = (f32[1,128,128]{2,1,0:T(8,128)S(1)}, f32[1,128,128]{2,1,0:T(8,128)}, u32[]{:S(2)}) copy-start(f32[1,128,128]{2,1,0:T(8,128)} %param.11) | copy-start | bytes 196612
Sparse Core Ops, SparseCore 0:
  11.2 77.8 all-gather.8
  120.9 69.8 all-reduce.6
  225.3 151.4 all-reduce.10
  459.6 69.4 all-gather.10
  563.1 69.9 all-reduce.8
  731.8 156.8 all-reduce.12
